TPU v7x, 32 devices: a whole 2x2x4 slice. The times are simulated.
32 devices in a mesh: dp: 2 (over x), expert: 16 (over z, y, core).
Axes of the slice: x: 2, y: 2, z: 4, core: 2. Of those that a mesh axis runs over, the one named last changes fastest.
Arguments:
- tokens: bfloat16 [8192, 1024], P(('dp', 'expert')), may hold values from -6 to 6
- modulation: bfloat16 [32, 2, 1024], P(('dp', 'expert')), may hold values from -3 to 3
- router_weight: bfloat16 [1024, 16], replicated, may hold values from -0.1875 to 0.1875
- weight_in: bfloat16 [16, 1024, 4096], P('expert', None, 'dp'), may hold values from -0.1875 to 0.1875
- weight_out: bfloat16 [16, 4096, 1024], P('expert', 'dp'), may hold values from -0.09375 to 0.09375
- chosen: int32 [2, 16, 256], P('dp'), may hold values from 0 to 4095, as said below
- grad_out: bfloat16 [8192, 1024], P(('dp', 'expert')), may hold values from -4 to 4
Outputs:
- grad_tokens: bfloat16 [8192, 1024], P(('dp', 'expert'))
- grad_mod: float32 [32, 2, 1024], P(('dp', 'expert'))
- grad_router: float32 [1024, 16], replicated
- grad_weight_in: bfloat16 [16, 1024, 4096], P('expert', None, 'dp')
- grad_weight_out: bfloat16 [16, 4096, 1024], P('expert', 'dp')
Inputs may be any that keep to these rules, and one draw needn't show every extreme that they name: `chosen`: for each slice and expert the 256 positions are distinct; at most 32 of them lie in one image's 256 tokens, and in one image exactly 32.
All inputs are finite; a program needn't handle non-finite values.
Results may differ from a plain program's by a relative error of at most 0.008.
Values may be sent and summed in bfloat16 or wider, within the bound.
No kernel may reach another device: no remote copies, remote signals or barrier semaphores. Data moves between devices by JAX's collectives and lax.ppermute only.
A program may use at most 128 MiB of HBM per device.

v0:
```python
import jax
import jax.numpy as jnp
from jax import lax
from jax.sharding import PartitionSpec as P

gelu_root = 0.7978845608028654
gelu_cube = 0.044715
norm_eps = 1e-06


def gelu_value(values):
    inner = gelu_root * (values + gelu_cube * values * values * values)
    return 0.5 * values * (1.0 + jnp.tanh(inner))


def gelu_slope(values):
    tangent = jnp.tanh(gelu_root * (values + gelu_cube * values * values * values))
    return 0.5 * (1.0 + tangent) + 0.5 * values * (1.0 - tangent * tangent) * gelu_root * (
        1.0 + 3.0 * gelu_cube * values * values
    )


def finish_terms(preact, upstream, rows_g, rows_p):
    hidden = gelu_value(preact).astype(jnp.bfloat16)
    score_sum = jnp.sum(hidden.astype(jnp.float32) * upstream, axis=1)
    prob_col = rows_p.astype(jnp.float32)[:, None]
    grad_y = (prob_col * rows_g.astype(jnp.float32)).astype(jnp.bfloat16)
    grad_pre = (prob_col * upstream * gelu_slope(preact)).astype(jnp.bfloat16)
    return (hidden, score_sum, grad_y, grad_pre)


def body(tokens, modulation, router_weight, weight_in, weight_out, chosen, grad_out):
    tok_count = tokens.shape[0]
    model_width = tokens.shape[1]
    experts = lax.axis_size("expert")
    my_index = lax.axis_index("expert")
    most_rows = 2 * tok_count // experts
    x_float = tokens.astype(jnp.float32)
    average = jnp.mean(x_float, axis=1, keepdims=True)
    centred = x_float - average
    spread = jnp.mean(centred * centred, axis=1, keepdims=True)
    inverse = lax.rsqrt(spread + norm_eps)
    normed = centred * inverse
    shift_mod = modulation[0, 0].astype(jnp.float32)
    scale_mod = modulation[0, 1].astype(jnp.float32)
    normal_u = (normed * (1.0 + scale_mod) + shift_mod).astype(jnp.bfloat16)
    gate_prob = jax.nn.sigmoid(
        jnp.dot(normal_u, router_weight, preferred_element_type=jnp.float32)
    ).astype(jnp.bfloat16)
    picked = chosen[0]
    local_row = picked - my_index * tok_count
    is_mine = (local_row >= 0) & (local_row < tok_count)
    rank_in = jnp.cumsum(is_mine.astype(jnp.int32), axis=1) - 1
    slot_at = jnp.where(is_mine, rank_in, most_rows)
    expert_col = jnp.arange(experts, dtype=jnp.int32)[:, None]
    rows_idx = (
        jnp.full((experts, most_rows), tok_count, jnp.int32)
        .at[expert_col, slot_at]
        .set(local_row, mode="drop")
    )
    u_pad = jnp.concatenate([normal_u, jnp.zeros((1, model_width), jnp.bfloat16)], axis=0)
    g_pad = jnp.concatenate([grad_out, jnp.zeros((1, model_width), jnp.bfloat16)], axis=0)
    p_pad = jnp.concatenate([gate_prob, jnp.zeros((1, experts), jnp.bfloat16)], axis=0)
    u_send = u_pad[rows_idx]
    g_send = g_pad[rows_idx]
    p_send = p_pad[rows_idx, expert_col]
    u_recv, g_recv, p_recv = (
        lax.all_to_all(u_send, "expert", split_axis=0, concat_axis=0, tiled=True),
        lax.all_to_all(g_send, "expert", split_axis=0, concat_axis=0, tiled=True),
        lax.all_to_all(p_send, "expert", split_axis=0, concat_axis=0, tiled=True),
    )
    u_all, g_all, p_all = (
        lax.all_gather(u_recv, "dp", axis=0, tiled=True),
        lax.all_gather(g_recv, "dp", axis=0, tiled=True),
        lax.all_gather(p_recv, "dp", axis=0, tiled=True),
    )
    rows_u = u_all.reshape(-1, model_width)
    rows_g = g_all.reshape(-1, model_width)
    rows_p = p_all.reshape(-1)
    first_w = weight_in[0]
    second_w = weight_out[0]
    preact = jnp.dot(rows_u, first_w, preferred_element_type=jnp.float32)
    upstream = lax.dot_general(
        rows_g, second_w, (((1,), (1,)), ((), ())), preferred_element_type=jnp.float32
    )
    hidden, score_sum, grad_y, grad_pre = finish_terms(preact, upstream, rows_g, rows_p)
    grad_first = lax.dot_general(
        rows_u, grad_pre, (((0,), (0,)), ((), ())), preferred_element_type=jnp.float32
    )
    grad_second = lax.dot_general(
        hidden, grad_y, (((0,), (0,)), ((), ())), preferred_element_type=jnp.float32
    )
    rows_part = lax.dot_general(
        grad_pre, first_w, (((1,), (1,)), ((), ())), preferred_element_type=jnp.float32
    )
    grad_sum, score_total = (
        lax.psum_scatter(
            rows_part.reshape(-1, most_rows, model_width), "dp", scatter_dimension=0, tiled=True
        ),
        lax.psum_scatter(score_sum.reshape(-1, most_rows), "dp", scatter_dimension=0, tiled=True),
    )
    grad_weight_in = grad_first.astype(jnp.bfloat16)[None]
    grad_weight_out = grad_second.astype(jnp.bfloat16)[None]
    grad_back = grad_sum.astype(jnp.bfloat16)
    score_back = score_total.astype(jnp.bfloat16)
    prob_recv = p_recv.astype(jnp.float32)
    logit_slots = score_back.astype(jnp.float32) * prob_recv * (1.0 - prob_recv)
    column = jnp.sum(u_recv.astype(jnp.float32) * logit_slots[:, :, None], axis=(0, 1))
    column = lax.psum(column, "dp")
    grad_router = lax.all_gather(column[:, None], "expert", axis=1, tiled=True)
    grad_ret, score_ret = (
        lax.all_to_all(grad_back, "expert", split_axis=0, concat_axis=0, tiled=True),
        lax.all_to_all(score_back, "expert", split_axis=0, concat_axis=0, tiled=True),
    )
    grad_u = (
        jnp.zeros((tok_count + 1, model_width), jnp.float32)
        .at[rows_idx]
        .add(grad_ret.astype(jnp.float32))[:tok_count]
    )
    prob_sent = p_send.astype(jnp.float32)
    logit_terms = score_ret.astype(jnp.float32) * prob_sent * (1.0 - prob_sent)
    grad_logit = (
        jnp.zeros((tok_count + 1, experts), jnp.float32)
        .at[rows_idx, expert_col]
        .add(logit_terms)[:tok_count]
    )
    grad_u = grad_u + jnp.dot(
        grad_logit, router_weight.astype(jnp.float32).T, precision=lax.Precision.HIGHEST
    )
    grad_shift = jnp.sum(grad_u, axis=0)
    grad_scale = jnp.sum(grad_u * normed, axis=0)
    grad_mod = jnp.stack([grad_shift, grad_scale], axis=0)[None]
    grad_norm = grad_u * (1.0 + scale_mod)
    centre_term = jnp.mean(grad_norm, axis=1, keepdims=True)
    slope_term = jnp.mean(grad_norm * normed, axis=1, keepdims=True)
    grad_tokens = (
        grad_out.astype(jnp.float32) + (grad_norm - centre_term - normed * slope_term) * inverse
    ).astype(jnp.bfloat16)
    return (grad_tokens, grad_mod, grad_router, grad_weight_in, grad_weight_out)


def solution(mesh):
    placed = (
        P(("dp", "expert"), None),
        P(("dp", "expert"), None, None),
        P(),
        P("expert", None, "dp"),
        P("expert", "dp", None),
        P("dp", None, None),
        P(("dp", "expert"), None),
    )
    return jax.shard_map(
        body,
        mesh=mesh,
        in_specs=placed,
        out_specs=(
            P(("dp", "expert"), None),
            P(("dp", "expert"), None, None),
            P(),
            P("expert", None, "dp"),
            P("expert", "dp", None),
        ),
        check_vma=False,
    )
```

profile of v0, /device:TPU:0, one launch (start us, length us, event | category | flops | bytes accessed | tf_op | source)
XLA Modules:
  0.0 315.4 jit_solution(3350218393936861215)
XLA Ops:
  8.6 0.7 subtract_bitcast_fusion
  9.3 0.7 fusion.44
  10.1 1.2 convert_reduce_fusion
  11.3 1.3 fusion.34
  13.6 0.7 and_reduce_fusion
  14.3 0.7 multiply_reduce_fusion.3
  15.1 15.5 %scatter_custom_fusion.2 = s32[512]{0:T(512)S(1)} fusion(s32[4096]{0:T(1024)S(1)} %bitcast.85, s32[4096]{0:T(1024)S(1)} %bitcast.84, s32[]{:T(128)} %constant.16.clone.1), kind=kCustom, calls=%fused_computation.83 | custom fusion | bytes 2052
  30.8 1.3 fusion.27
  32.2 2.1 gather_fusion.2
  34.2 32.0 %all_to_all.37 = bf16[16,32,1024]{2,1,0:T(8,128)(2,1)} all-to-all(bf16[16,32,1024]{2,1,0:T(8,128)(2,1)S(1)} %bitcast.75), channel_id=1, replica_groups=mesh['dp'=2,'expert'=16] {'expert'}, dimensions={0} | all-to-all | bytes 2097152 | tf_op jit(solution)/shard_map/all_to_all | solution.py:68
  66.4 2.1 gather_fusion.1
  68.4 29.6 %all_to_all.38 = bf16[16,32,1024]{2,1,0:T(8,128)(2,1)} all-to-all(bf16[16,32,1024]{2,1,0:T(8,128)(2,1)S(1)} %bitcast.74), channel_id=1, replica_groups=mesh['dp'=2,'expert'=16] {'expert'}, dimensions={0} | all-to-all | bytes 2097152 | tf_op jit(solution)/shard_map/all_to_all | solution.py:69
  98.5 4.9 %gather_fusion = bf16[512]{0:T(512)(128)(2,1)S(1)} fusion(bf16[257,16]{0,1:T(8,128)(2,1)S(1)} %concatenate.17, s32[512]{0:T(512)S(1)} %reshape.169), kind=kCustom, calls=%fused_computation | custom fusion | bytes 6144 | tf_op jit(solution)/shard_map/gather | solution.py:66
  103.5 11.3 %all_to_all.39 = bf16[16,1,32]{2,1,0:T(2,128)(2,1)S(1)} all-to-all(bf16[16,1,32]{2,1,0:T(2,128)(2,1)S(1)} %all_to_all.31), channel_id=1, replica_groups=mesh['dp'=2,'expert'=16] {'expert'}, dimensions={0} | all-to-all | bytes 2048 | tf_op jit(solution)/shard_map/all_to_all | solution.py:70
  114.8 4.7 %all-gather = bf16[32,1,32]{2,0,1:T(8,128)(2,1)S(1)} all-gather(bf16[16,1,32]{2,0,1:T(8,128)(2,1)S(1)} %copy.27), channel_id=2, replica_groups=mesh['dp'=2,'expert'=16] {'dp'}, dimensions={0}, use_global_device_ids=true | all-gather | bytes 3072 | tf_op jit(solution)/shard_map/all_gather | solution.py:75
  119.6 10.5 %fusion.9 = f32[1024,2048]{1,0:T(8,128)} fusion(bf16[1024,1024]{1,0:T(8,128)(2,1)} %bitcast.88, bf16[1,1024,2048]{2,1,0:T(8,128)(2,1)} %param.10), kind=kOutput, calls=%fused_computation.19 | convolution fusion | flops 4294967296 | bytes 14680064 | tf_op jit(solution)/shard_map/dot_general | solution.py:82
  130.1 4.5 %all-gather.5.cloned.1.call-done = bf16[32,32,1024]{2,1,0:T(8,128)(2,1)} async-done(((bf16[16,32,1024]{2,1,0:T(8,128)(2,1)}), bf16[32,32,1024]{2,1,0:T(8,128)(2,1)}) %all-gather.5.cloned.1.call-update) | async-done | bytes 2097168 | tf_op jit(solution)/shard_map/all_gather | solution.py:74
  134.6 14.5 %multiply_reduce_fusion = (f32[1024]{0:T(1024)S(1)}, bf16[1024,2048]{1,0:T(8,128)(2,1)}) fusion(f32[1024,2048]{1,0:T(8,128)} %fusion.9, f32[1024]{0:T(1024)S(1)} %reshape.167, bf16[1024,1024]{1,0:T(8,128)(2,1)} %bitcast.90, bf16[1,2048,1024]{2,1,0:T(8,128)(2,1)} %param.11), kind=kOutput, calls=%fused_computation.15 | convolution fusion | flops 4347395072 | bytes 18882560 | tf_op jit(solution)/shard_map/dot_general | solution.py:83
  149.9 10.0 %fusion.7 = f32[32,32,1024]{2,1,0:T(8,128)} fusion(bf16[32,32,2048]{2,1,0:T(8,128)(2,1)} %bitcast.92, bf16[1,1024,2048]{2,1,0:T(8,128)(2,1)} %param.10), kind=kOutput, calls=%fused_computation.17 | convolution fusion | flops 4294967296 | bytes 12582912 | tf_op jit(solution)/shard_map/dot_general | solution.py:93
  160.0 0.7 subtract_multiply_fusion
  161.3 5.6 %all-to-all-start.4 = ((bf16[16,1,32]{2,1,0:T(2,128)(2,1)}), bf16[16,1,32]{2,1,0:T(2,128)(2,1)S(1)}, u32[]{:S(2)}, u32[]{:S(2)}) async-start(bf16[16,1,32]{2,1,0:T(2,128)(2,1)} %copy.28), calls=%async_computation.6 | async-start | bytes 16384 | tf_op jit(solution)/shard_map/all_to_all | solution.py:113
  167.1 50.0 %reduce-scatter.3.cloned.1.call-done = f32[16,32,1024]{2,1,0:T(8,128)} async-done(((f32[32,32,1024]{2,1,0:T(8,128)}), f32[16,32,1024]{2,1,0:T(8,128)}) %reduce-scatter.3.cloned.1.call-update) | async-done | bytes 2097168 | tf_op jit(solution)/shard_map/reduce_scatter | solution.py:97
  217.1 2.8 convert_element_type.111
  219.8 5.6 %all-to-all-start.3 = ((bf16[16,32,1024]{2,1,0:T(8,128)(2,1)}), bf16[16,32,1024]{2,1,0:T(8,128)(2,1)S(1)}, u32[]{:S(2)}, u32[]{:S(2)}) async-start(bf16[16,32,1024]{2,1,0:T(8,128)(2,1)} %convert_element_type.111), calls=%async_computation.4 | async-start | bytes 2097152 | tf_op jit(solution)/shard_map/all_to_all | solution.py:112
  225.5 9.6 %convert_bitcast_fusion.1 = bf16[1,1024,2048]{2,1,0:T(8,128)(2,1)} fusion(bf16[1024,1024]{1,0:T(8,128)(2,1)} %bitcast.89, bf16[1024,2048]{1,0:T(8,128)(2,1)} %get-tuple-element.12), kind=kOutput, calls=%fused_computation.25 | convolution fusion | flops 4297064448 | bytes 10485760 | tf_op jit(solution)/shard_map/dot_general | solution.py:87
  235.0 11.7 %convert_bitcast_fusion = bf16[1,2048,1024]{2,1,0:T(8,128)(2,1)} fusion(bf16[1024,1024]{1,0:T(8,128)(2,1)S(1)} %bitcast.91, f32[1024]{0:T(1024)S(1)} %reshape.167, f32[1024,2048]{1,0:T(8,128)} %fusion.9), kind=kOutput, calls=%fused_computation.23 | convolution fusion | flops 4319084544 | bytes 14684160 | tf_op jit(solution)/shard_map/dot_general | solution.py:90
  247.0 4.9 %psum.7 = f32[1024,1]{0,1:T(1,128)S(1)} all-reduce(f32[1024,1]{0,1:T(1,128)S(1)} %bitcast.82), channel_id=1, replica_groups=mesh['dp'=2,'expert'=16] {'dp'}, use_global_device_ids=true, to_apply=%region_15.16 | all-reduce | flops 1024 | bytes 8192 | tf_op jit(solution)/shard_map/psum | solution.py:109
  252.0 22.1 %all-gather.1 = f32[16,1,1024]{2,1,0:T(1,128)S(1)} all-gather(f32[1,1,1024]{2,1,0:T(1,128)S(1)} %bitcast.83), channel_id=1, replica_groups=mesh['dp'=2,'expert'=16] {'expert'}, dimensions={0}, use_global_device_ids=true | all-gather | bytes 69632 | tf_op jit(solution)/shard_map/all_gather | solution.py:110
  274.8 25.9 %scatter_fusion = f32[257,16]{0,1:T(8,128)S(1)} fusion(f32[257,16]{0,1:T(8,128)S(1)} %broadcast_in_dim.30, s32[512]{0:T(512)S(1)} %reshape.199, f32[512]{0:T(512)S(1)} %reshape.201), kind=kCustom, calls=%fused_computation.4 | custom fusion | flops 512 | bytes 10240 | tf_op jit(solution)/shard_map/scatter-add | solution.py:125
  300.7 5.1 %scatter_custom_fusion = f32[257,1024]{1,0:T(8,128)S(1)} fusion(s32[512]{0:T(512)S(1)} %reshape.193, bf16[512,1024]{1,0:T(8,128)(2,1)S(1)} %bitcast.73, f32[]{:T(128)} %constant.15.clone.1), kind=kCustom, calls=%fused_computation.26 | custom fusion | flops 1048576 | bytes 2101252 | tf_op jit(solution)/shard_map/scatter-add | solution.py:118
  305.8 1.1 fusion.33
  307.6 1.3 fusion.32
  (65 shorter events, 6.5 us)
Async XLA Ops:
  7.2 91.0 %copy-start = (bf16[1024,16]{0,1:T(8,128)(2,1)S(1)}, bf16[1024,16]{0,1:T(8,128)(2,1)}, u32[]{:S(2)}) copy-start(bf16[1024,16]{0,1:T(8,128)(2,1)} %param.9) | copy-start | bytes 98308
  7.2 112.4 %all-gather.7.cloned.1.call-start = ((), (), s32[]{:S(2)}) async-start(), calls=%async_computation.8 | async-start | bytes 3145728 | tf_op jit(solution)/shard_map/all_gather | solution.py:73
  32.1 34.2 %copy-start.3 = (bf16[256,1024]{1,0:T(8,128)(2,1)S(1)}, bf16[256,1024]{1,0:T(8,128)(2,1)}, u32[]{:S(2)}) copy-start(bf16[256,1024]{1,0:T(8,128)(2,1)} %param.13) | copy-start | bytes 1572868
  66.3 68.4 %all-gather.5.cloned.1.call-start = ((), (), s32[]{:S(2)}) async-start(), calls=%async_computation.7 | async-start | bytes 3145728 | tf_op jit(solution)/shard_map/all_gather | solution.py:74
  98.1 61.9 %reduce-scatter.5.cloned.1.call-start = ((), (), s32[]{:S(2)}) async-start(), calls=%async_computation.10 | async-start | bytes 24576 | tf_op jit(solution)/shard_map/reduce_scatter | solution.py:100
  149.8 67.2 %reduce-scatter.3.cloned.1.call-start = ((), (), s32[]{:S(2)}) async-start(), calls=%async_computation.9 | async-start | bytes 6291456 | tf_op jit(solution)/shard_map/reduce_scatter | solution.py:97
  161.3 58.6 %all-to-all-start.4 = ((bf16[16,1,32]{2,1,0:T(2,128)(2,1)}), bf16[16,1,32]{2,1,0:T(2,128)(2,1)S(1)}, u32[]{:S(2)}, u32[]{:S(2)}) async-start(bf16[16,1,32]{2,1,0:T(2,128)(2,1)} %copy.28), calls=%async_computation.6 | async-start | bytes 16384 | tf_op jit(solution)/shard_map/all_to_all | solution.py:113
  219.8 80.9 %all-to-all-start.3 = ((bf16[16,32,1024]{2,1,0:T(8,128)(2,1)}), bf16[16,32,1024]{2,1,0:T(8,128)(2,1)S(1)}, u32[]{:S(2)}, u32[]{:S(2)}) async-start(bf16[16,32,1024]{2,1,0:T(8,128)(2,1)} %convert_element_type.111), calls=%async_computation.4 | async-start | bytes 2097152 | tf_op jit(solution)/shard_map/all_to_all | solution.py:112
  225.5 9.6 %copy-start.4 = (bf16[32,32,1024]{2,1,0:T(8,128)(2,1)S(1)}, bf16[32,32,1024]{2,1,0:T(8,128)(2,1)}, u32[]{:S(2)}) copy-start(bf16[32,32,1024]{2,1,0:T(8,128)(2,1)} %all-gather.5.cloned.1.call-done) | copy-start | bytes 6291460
  235.0 11.7 %copy-start.1 = (bf16[16,32,1024]{2,1,0:T(8,128)(2,1)S(1)}, bf16[16,32,1024]{2,1,0:T(8,128)(2,1)}, u32[]{:S(2)}) copy-start(bf16[16,32,1024]{2,1,0:T(8,128)(2,1)} %all_to_all.37) | copy-start | bytes 3145732
  274.8 31.0 %copy-start.2 = (bf16[256,1024]{1,0:T(8,128)(2,1)S(1)}, bf16[256,1024]{1,0:T(8,128)(2,1)}, u32[]{:S(2)}) copy-start(bf16[256,1024]{1,0:T(8,128)(2,1)} %param.7) | copy-start | bytes 1572868
Sparse Core Ops, SparseCore 0:
  66.4 33.4 all-gather.6
  101.4 33.1 all-gather.4
  150.0 9.9 reduce-scatter.4
  162.7 54.3 reduce-scatter.2
where the time goes:
time: 316 us; the launch traced here: 315 us
  blocking collectives  105 us (33%)
  matrix products  57.7 us (18%)
  waiting for transfers between devices  54.6 us (17%)
  other arithmetic  45.5 us (14%)
  local copies, waits for them, and re-layouts  27.5 us (9%)
  between operations  14 us (4%)
  starting transfers between devices  11.4 us (4%)
    reduce_scatter x1, waiting for transfers between devices, body(): lax.psum_scatter(rows_part.reshape(-1, most_rows, model_width), 'dp', sca...  50 us
    all_to_all x1, blocking collectives, body(): lax.all_to_all(u_send, 'expert', split_axis=0, concat_axis=0, tiled=True)  32 us
    all_to_all x1, blocking collectives, body(): lax.all_to_all(g_send, 'expert', split_axis=0, concat_axis=0, tiled=True)  29.6 us
    scatter-add x1, other arithmetic, body(): grad_logit = jnp.zeros((tok_count + 1, experts), jnp.float32).at[rows_idx...  25.9 us
    all_gather x1, blocking collectives, body(): grad_router = lax.all_gather(column[:, None], 'expert', axis=1, tiled=True)  22.1 us
    unnamed x14, local copies, waits for them, and re-layouts  16.2 us
    dot_general x1, matrix products, body(): lax.dot_general(rows_g, second_w, (((1,), (1,)), ((), ())), preferred_ele...  14.5 us
    dot_general x1, matrix products, body(): lax.dot_general(hidden, grad_y, (((0,), (0,)), ((), ())), preferred_eleme...  11.7 us
  transfers between devices with their start and end apart: 6, of which 2 were waited for; matrix products, arithmetic and copies ran while one was open for 25% of the time, Pallas kernels for 0%

commit v1 on v0

--- a/solution.py
+++ b/solution.py
@@ -6,6 +6,19 @@
 gelu_root = 0.7978845608028654
 gelu_cube = 0.044715
 norm_eps = 1e-06
+
+
+def collect(x, axis, dim):
+    ways = lax.axis_size(axis)
+    up = [(d, (d + 1) % ways) for d in range(ways)]
+    down = [(d, (d - 1) % ways) for d in range(ways)]
+    earlier, later = ([x], [x])
+    for _ in range(ways // 2):
+        earlier.append(lax.ppermute(earlier[-1], axis, up))
+    for _ in range((ways - 1) // 2):
+        later.append(lax.ppermute(later[-1], axis, down))
+    line = jnp.concatenate([*earlier[::-1], *later[1:]], axis=dim)
+    return jnp.roll(line, (lax.axis_index(axis) - ways // 2) * x.shape[dim], axis=dim)
 
 
 def gelu_value(values):
@@ -107,7 +120,7 @@
     logit_slots = score_back.astype(jnp.float32) * prob_recv * (1.0 - prob_recv)
     column = jnp.sum(u_recv.astype(jnp.float32) * logit_slots[:, :, None], axis=(0, 1))
     column = lax.psum(column, "dp")
-    grad_router = lax.all_gather(column[:, None], "expert", axis=1, tiled=True)
+    grad_router = collect(column[:, None], "expert", 1)
     grad_ret, score_ret = (
         lax.all_to_all(grad_back, "expert", split_axis=0, concat_axis=0, tiled=True),
         lax.all_to_all(score_back, "expert", split_axis=0, concat_axis=0, tiled=True),

time: 316 us -> 295 us (0.934)
  starting transfers between devices: 11.4 us -> 42.4 us
  waiting for transfers between devices: 54.6 us -> 26.7 us
  blocking collectives: 105 us -> 82.5 us
    reduce_scatter x1, waiting for transfers between devices: 50 us -> 16.8 us  [body(): lax.psum_scatter(rows_part.reshape(-1, most_rows, model_width), 'dp', sca...]
    ppermute x0 -> x15, starting transfers between devices: none -> 30.8 us  [the longest x7 30.7 us: collect(): later.append(lax.ppermute(later[-1], axis, down))]
    all_gather x1 -> x0, blocking collectives: 22.1 us -> none  [body(): grad_router = lax.all_gather(column[:, None], 'expert', axis=1, tiled=True)]
    ppermute x0 -> x15, waiting for transfers between devices: none -> 5.28 us  [the longest x8 5.14 us: collect(): earlier.append(lax.ppermute(earlier[-1], axis, up))]
    dot_general x1, matrix products: 9.56 us -> 6.12 us  [body(): lax.dot_general(rows_u, grad_pre, (((0,), (0,)), ((), ())), preferred_ele...]
    unnamed x14 -> x15, local copies, waits for them, and re-layouts: 16.2 us -> 15.9 us
  transfers between devices with their start and end apart: 6 -> 21, of which waited for: 2 -> 6; matrix products, arithmetic and copies ran while one was open for 25% -> 26% of each run, Pallas kernels for 0% -> 0%
where the time goes in v1:
time: 295 us; the launch traced here: 294 us
  blocking collectives  82.5 us (28%)
  matrix products  54.9 us (19%)
  other arithmetic  45.5 us (15%)
  starting transfers between devices  42.4 us (14%)
  local copies, waits for them, and re-layouts  28.1 us (10%)
  waiting for transfers between devices  26.7 us (9%)
  between operations  14.1 us (5%)
    all_to_all x1, blocking collectives, body(): lax.all_to_all(u_send, 'expert', split_axis=0, concat_axis=0, tiled=True)  32 us
    ppermute x7, starting transfers between devices, collect(): later.append(lax.ppermute(later[-1], axis, down))  30.7 us
    all_to_all x1, blocking collectives, body(): lax.all_to_all(g_send, 'expert', split_axis=0, concat_axis=0, tiled=True)  29.6 us
    scatter-add x1, other arithmetic, body(): grad_logit = jnp.zeros((tok_count + 1, experts), jnp.float32).at[rows_idx...  25.9 us
    reduce_scatter x1, waiting for transfers between devices, body(): lax.psum_scatter(rows_part.reshape(-1, most_rows, model_width), 'dp', sca...  16.8 us
    unnamed x15, local copies, waits for them, and re-layouts  15.9 us
    dot_general x1, matrix products, body(): lax.dot_general(rows_g, second_w, (((1,), (1,)), ((), ())), preferred_ele...  14.5 us
    dot_general x1, matrix products, body(): lax.dot_general(hidden, grad_y, (((0,), (0,)), ((), ())), preferred_eleme...  12.4 us
  transfers between devices with their start and end apart: 21, of which 6 were waited for; matrix products, arithmetic and copies ran while one was open for 26% of the time, Pallas kernels for 0%

profile of v1, /device:TPU:0, one launch (start us, length us, event | category | flops | bytes accessed | tf_op | source)
XLA Modules:
  0.0 294.3 jit_solution(7245434862311014210)
XLA Ops:
  11.3 1.3 fusion.34
  15.1 15.5 %scatter_custom_fusion.2 = s32[512]{0:T(512)S(1)} fusion(s32[4096]{0:T(1024)S(1)} %bitcast.77, s32[4096]{0:T(1024)S(1)} %bitcast.76, s32[]{:T(128)} %constant.24.clone.1), kind=kCustom, calls=%fused_computation.82 | custom fusion | bytes 2052
  30.8 1.3 fusion.27
  32.2 2.1 gather_fusion.2
  34.2 32.0 %all_to_all.37 = bf16[16,32,1024]{2,1,0:T(8,128)(2,1)} all-to-all(bf16[16,32,1024]{2,1,0:T(8,128)(2,1)S(1)} %bitcast.69), channel_id=1, replica_groups=mesh['dp'=2,'expert'=16] {'expert'}, dimensions={0} | all-to-all | bytes 2097152 | tf_op jit(solution)/shard_map/all_to_all | solution.py:81
  66.4 2.1 gather_fusion.1
  68.4 29.6 %all_to_all.38 = bf16[16,32,1024]{2,1,0:T(8,128)(2,1)} all-to-all(bf16[16,32,1024]{2,1,0:T(8,128)(2,1)S(1)} %bitcast.68), channel_id=1, replica_groups=mesh['dp'=2,'expert'=16] {'expert'}, dimensions={0} | all-to-all | bytes 2097152 | tf_op jit(solution)/shard_map/all_to_all | solution.py:82
  98.5 4.9 %gather_fusion = bf16[512]{0:T(512)(128)(2,1)S(1)} fusion(bf16[257,16]{0,1:T(8,128)(2,1)S(1)} %concatenate.23, s32[512]{0:T(512)S(1)} %reshape.169), kind=kCustom, calls=%fused_computation | custom fusion | bytes 6144 | tf_op jit(solution)/shard_map/gather | solution.py:79
  103.5 11.3 %all_to_all.39 = bf16[16,1,32]{2,1,0:T(2,128)(2,1)S(1)} all-to-all(bf16[16,1,32]{2,1,0:T(2,128)(2,1)S(1)} %all_to_all.31), channel_id=1, replica_groups=mesh['dp'=2,'expert'=16] {'expert'}, dimensions={0} | all-to-all | bytes 2048 | tf_op jit(solution)/shard_map/all_to_all | solution.py:83
  114.8 4.7 %all-gather = bf16[32,1,32]{2,0,1:T(8,128)(2,1)S(1)} all-gather(bf16[16,1,32]{2,0,1:T(8,128)(2,1)S(1)} %copy.27), channel_id=2, replica_groups=mesh['dp'=2,'expert'=16] {'dp'}, dimensions={0}, use_global_device_ids=true | all-gather | bytes 3072 | tf_op jit(solution)/shard_map/all_gather | solution.py:88
  119.6 10.5 %fusion.9 = f32[1024,2048]{1,0:T(8,128)} fusion(bf16[1024,1024]{1,0:T(8,128)(2,1)} %bitcast.80, bf16[1,1024,2048]{2,1,0:T(8,128)(2,1)} %param.10), kind=kOutput, calls=%fused_computation.19 | convolution fusion | flops 4294967296 | bytes 14680064 | tf_op jit(solution)/shard_map/dot_general | solution.py:95
  130.1 4.5 %all-gather.4.cloned.1.call-done = bf16[32,32,1024]{2,1,0:T(8,128)(2,1)} async-done(((bf16[16,32,1024]{2,1,0:T(8,128)(2,1)}), bf16[32,32,1024]{2,1,0:T(8,128)(2,1)}) %all-gather.4.cloned.1.call-update) | async-done | bytes 2097168 | tf_op jit(solution)/shard_map/all_gather | solution.py:87
  134.6 14.5 %multiply_reduce_fusion = (f32[1024]{0:T(1024)S(1)}, bf16[1024,2048]{1,0:T(8,128)(2,1)}) fusion(f32[1024,2048]{1,0:T(8,128)} %fusion.9, f32[1024]{0:T(1024)S(1)} %reshape.167, bf16[1024,1024]{1,0:T(8,128)(2,1)} %bitcast.82, bf16[1,2048,1024]{2,1,0:T(8,128)(2,1)} %param.11), kind=kOutput, calls=%fused_computation.15 | convolution fusion | flops 4347395072 | bytes 18882560 | tf_op jit(solution)/shard_map/dot_general | solution.py:96
  149.9 10.0 %fusion.7 = f32[32,32,1024]{2,1,0:T(8,128)} fusion(bf16[32,32,2048]{2,1,0:T(8,128)(2,1)} %bitcast.84, bf16[1,1024,2048]{2,1,0:T(8,128)(2,1)} %param.10), kind=kOutput, calls=%fused_computation.17 | convolution fusion | flops 4294967296 | bytes 12582912 | tf_op jit(solution)/shard_map/dot_general | solution.py:106
  161.4 4.9 %psum.7 = f32[1024,1]{0,1:T(1,128)S(1)} all-reduce(f32[1024,1]{0,1:T(1,128)S(1)} %bitcast.75), channel_id=1, replica_groups=mesh['dp'=2,'expert'=16] {'dp'}, use_global_device_ids=true, to_apply=%region_15.16 | all-reduce | flops 1024 | bytes 8192 | tf_op jit(solution)/shard_map/psum | solution.py:122
  166.3 4.4 %collective-permute-start.8 = (f32[1024,1]{0,1:T(1,128)S(1)}, f32[1024,1]{0,1:T(1,128)S(1)}, u32[]{:S(2)}, u32[]{:S(2)}) collective-permute-start(f32[1024,1]{0,1:T(1,128)S(1)} %psum.7), channel_id=1, source_target_pairs={{0,15},{1,0},{2,1},{3,2},{4,3},{5,4},{6,5},{7,6},{8,7},{9,8},{10,9... | collective-permute-start | bytes 12296 | tf_op jit(solution)/shard_map/ppermute | solution.py:19
  170.8 1.3 collective-permute-done
  172.1 4.4 %collective-permute-start.9 = (f32[1024,1]{0,1:T(1,128)S(1)}, f32[1024,1]{0,1:T(1,128)S(1)}, u32[]{:S(2)}, u32[]{:S(2)}) collective-permute-start(f32[1024,1]{0,1:T(1,128)S(1)} %collective-permute-done.8), channel_id=1, source_target_pairs={{0,15},{1,0},{2,1},{3,2},{4,3},{5,4},{6,5},{7,6},{8,7},{9,8},{10,9... | collective-permute-start | bytes 12296 | tf_op jit(solution)/shard_map/ppermute | solution.py:19
  176.5 1.3 collective-permute-done.1
  177.9 4.4 %collective-permute-start.10 = (f32[1024,1]{0,1:T(1,128)S(1)}, f32[1024,1]{0,1:T(1,128)S(1)}, u32[]{:S(2)}, u32[]{:S(2)}) collective-permute-start(f32[1024,1]{0,1:T(1,128)S(1)} %collective-permute-done.9), channel_id=1, source_target_pairs={{0,15},{1,0},{2,1},{3,2},{4,3},{5,4},{6,5},{7,6},{8,7},{9,8},{10,9... | collective-permute-start | bytes 12296 | tf_op jit(solution)/shard_map/ppermute | solution.py:19
  183.6 4.4 %collective-permute-start.11 = (f32[1024,1]{0,1:T(1,128)S(1)}, f32[1024,1]{0,1:T(1,128)S(1)}, u32[]{:S(2)}, u32[]{:S(2)}) collective-permute-start(f32[1024,1]{0,1:T(1,128)S(1)} %collective-permute-done.10), channel_id=1, source_target_pairs={{0,15},{1,0},{2,1},{3,2},{4,3},{5,4},{6,5},{7,6},{8,7},{9,8},{10,9... | collective-permute-start | bytes 12296 | tf_op jit(solution)/shard_map/ppermute | solution.py:19
  189.9 5.8 %all-to-all-start.4 = ((bf16[16,1,32]{2,1,0:T(2,128)(2,1)}), bf16[16,1,32]{2,1,0:T(2,128)(2,1)S(1)}, u32[]{:S(2)}, u32[]{:S(2)}) async-start(bf16[16,1,32]{2,1,0:T(2,128)(2,1)} %copy.28), calls=%async_computation.6 | async-start | bytes 16384 | tf_op jit(solution)/shard_map/all_to_all | solution.py:126
  195.9 4.3 %collective-permute-start.12 = (f32[1024,1]{0,1:T(1,128)S(1)}, f32[1024,1]{0,1:T(1,128)S(1)}, u32[]{:S(2)}, u32[]{:S(2)}) collective-permute-start(f32[1024,1]{0,1:T(1,128)S(1)} %collective-permute-done.11), channel_id=1, source_target_pairs={{0,15},{1,0},{2,1},{3,2},{4,3},{5,4},{6,5},{7,6},{8,7},{9,8},{10,9... | collective-permute-start | bytes 12296 | tf_op jit(solution)/shard_map/ppermute | solution.py:19
  200.2 16.8 %reduce-scatter.3.cloned.1.call-done = f32[16,32,1024]{2,1,0:T(8,128)} async-done(((f32[32,32,1024]{2,1,0:T(8,128)}), f32[16,32,1024]{2,1,0:T(8,128)}) %reduce-scatter.3.cloned.1.call-update) | async-done | bytes 2097168 | tf_op jit(solution)/shard_map/reduce_scatter | solution.py:110
  217.1 2.7 convert_element_type.111
  219.8 5.6 %all-to-all-start.3 = ((bf16[16,32,1024]{2,1,0:T(8,128)(2,1)}), bf16[16,32,1024]{2,1,0:T(8,128)(2,1)S(1)}, u32[]{:S(2)}, u32[]{:S(2)}) async-start(bf16[16,32,1024]{2,1,0:T(8,128)(2,1)} %convert_element_type.111), calls=%async_computation.4 | async-start | bytes 2097152 | tf_op jit(solution)/shard_map/all_to_all | solution.py:125
  225.4 12.4 %convert_bitcast_fusion = bf16[1,2048,1024]{2,1,0:T(8,128)(2,1)} fusion(bf16[1024,1024]{1,0:T(8,128)(2,1)} %bitcast.83, f32[1024]{0:T(1024)S(1)} %reshape.167, f32[1024,2048]{1,0:T(8,128)} %fusion.9), kind=kOutput, calls=%fused_computation.23 | convolution fusion | flops 4319084544 | bytes 14684160 | tf_op jit(solution)/shard_map/dot_general | solution.py:103
  237.8 4.3 %collective-permute-start.13 = (f32[1024,1]{0,1:T(1,128)S(1)}, f32[1024,1]{0,1:T(1,128)S(1)}, u32[]{:S(2)}, u32[]{:S(2)}) collective-permute-start(f32[1024,1]{0,1:T(1,128)S(1)} %collective-permute-done.12), channel_id=1, source_target_pairs={{0,15},{1,0},{2,1},{3,2},{4,3},{5,4},{6,5},{7,6},{8,7},{9,8},{10,9... | collective-permute-start | bytes 12296 | tf_op jit(solution)/shard_map/ppermute | solution.py:19
  242.2 6.1 %convert_bitcast_fusion.1 = bf16[1,1024,2048]{2,1,0:T(8,128)(2,1)} fusion(bf16[1024,1024]{1,0:T(8,128)(2,1)S(1)} %bitcast.81, bf16[1024,2048]{1,0:T(8,128)(2,1)S(1)} %copy-done.5), kind=kOutput, calls=%fused_computation.25 | convolution fusion | flops 4297064448 | bytes 10485760 | tf_op jit(solution)/shard_map/dot_general | solution.py:100
  248.3 4.4 %collective-permute-start.14 = (f32[1024,1]{0,1:T(1,128)S(1)}, f32[1024,1]{0,1:T(1,128)S(1)}, u32[]{:S(2)}, u32[]{:S(2)}) collective-permute-start(f32[1024,1]{0,1:T(1,128)S(1)} %collective-permute-done.13), channel_id=1, source_target_pairs={{0,15},{1,0},{2,1},{3,2},{4,3},{5,4},{6,5},{7,6},{8,7},{9,8},{10,9... | collective-permute-start | bytes 12296 | tf_op jit(solution)/shard_map/ppermute | solution.py:19
  252.8 25.9 %scatter_fusion = f32[257,16]{0,1:T(8,128)S(1)} fusion(f32[257,16]{0,1:T(8,128)S(1)} %broadcast_in_dim.30, s32[512]{0:T(512)S(1)} %reshape.199, f32[512]{0:T(512)S(1)} %reshape.201), kind=kCustom, calls=%fused_computation.4 | custom fusion | flops 512 | bytes 10240 | tf_op jit(solution)/shard_map/scatter-add | solution.py:138
  279.7 5.1 %scatter_custom_fusion = f32[257,1024]{1,0:T(8,128)S(1)} fusion(s32[512]{0:T(512)S(1)} %reshape.193, bf16[512,1024]{1,0:T(8,128)(2,1)S(1)} %bitcast.67, f32[]{:T(128)} %constant.23.clone.1), kind=kCustom, calls=%fused_computation.26 | custom fusion | flops 1048576 | bytes 2101252 | tf_op jit(solution)/shard_map/scatter-add | solution.py:131
  (97 shorter events, 17.1 us)
Async XLA Ops:
  7.2 91.0 %copy-start = (bf16[1024,16]{0,1:T(8,128)(2,1)S(1)}, bf16[1024,16]{0,1:T(8,128)(2,1)}, u32[]{:S(2)}) copy-start(bf16[1024,16]{0,1:T(8,128)(2,1)} %param.9) | copy-start | bytes 98308
  7.2 112.4 %all-gather.6.cloned.1.call-start = ((), (), s32[]{:S(2)}) async-start(), calls=%async_computation.8 | async-start | bytes 3145728 | tf_op jit(solution)/shard_map/all_gather | solution.py:86
  32.1 34.2 %copy-start.3 = (bf16[256,1024]{1,0:T(8,128)(2,1)S(1)}, bf16[256,1024]{1,0:T(8,128)(2,1)}, u32[]{:S(2)}) copy-start(bf16[256,1024]{1,0:T(8,128)(2,1)} %param.13) | copy-start | bytes 1572868
  66.3 68.4 %all-gather.4.cloned.1.call-start = ((), (), s32[]{:S(2)}) async-start(), calls=%async_computation.7 | async-start | bytes 3145728 | tf_op jit(solution)/shard_map/all_gather | solution.py:87
  98.1 61.9 %reduce-scatter.5.cloned.1.call-start = ((), (), s32[]{:S(2)}) async-start(), calls=%async_computation.10 | async-start | bytes 24576 | tf_op jit(solution)/shard_map/reduce_scatter | solution.py:113
  149.8 67.2 %reduce-scatter.3.cloned.1.call-start = ((), (), s32[]{:S(2)}) async-start(), calls=%async_computation.9 | async-start | bytes 6291456 | tf_op jit(solution)/shard_map/reduce_scatter | solution.py:110
  159.9 1.2 copy-start.1
  166.3 5.7 %collective-permute-start = (f32[1024,1]{0,1:T(1,128)S(1)}, f32[1024,1]{0,1:T(1,128)S(1)}, u32[]{:S(2)}, u32[]{:S(2)}) collective-permute-start(f32[1024,1]{0,1:T(1,128)S(1)} %psum.7), channel_id=1, source_target_pairs={{0,1},{1,2},{2,3},{3,4},{4,5},{5,6},{6,7},{7,8},{8,9},{9,10},{10,1... | collective-permute-start | bytes 12296 | tf_op jit(solution)/shard_map/ppermute | solution.py:17
  166.3 5.8 %collective-permute-start.8 = (f32[1024,1]{0,1:T(1,128)S(1)}, f32[1024,1]{0,1:T(1,128)S(1)}, u32[]{:S(2)}, u32[]{:S(2)}) collective-permute-start(f32[1024,1]{0,1:T(1,128)S(1)} %psum.7), channel_id=1, source_target_pairs={{0,15},{1,0},{2,1},{3,2},{4,3},{5,4},{6,5},{7,6},{8,7},{9,8},{10,9... | collective-permute-start | bytes 12296 | tf_op jit(solution)/shard_map/ppermute | solution.py:19
  172.1 5.7 %collective-permute-start.1 = (f32[1024,1]{0,1:T(1,128)S(1)}, f32[1024,1]{0,1:T(1,128)S(1)}, u32[]{:S(2)}, u32[]{:S(2)}) collective-permute-start(f32[1024,1]{0,1:T(1,128)S(1)} %collective-permute-done), channel_id=1, source_target_pairs={{0,1},{1,2},{2,3},{3,4},{4,5},{5,6},{6,7},{7,8},{8,9},{9,10},{10,1... | collective-permute-start | bytes 12296 | tf_op jit(solution)/shard_map/ppermute | solution.py:17
  172.1 5.7 %collective-permute-start.9 = (f32[1024,1]{0,1:T(1,128)S(1)}, f32[1024,1]{0,1:T(1,128)S(1)}, u32[]{:S(2)}, u32[]{:S(2)}) collective-permute-start(f32[1024,1]{0,1:T(1,128)S(1)} %collective-permute-done.8), channel_id=1, source_target_pairs={{0,15},{1,0},{2,1},{3,2},{4,3},{5,4},{6,5},{7,6},{8,7},{9,8},{10,9... | collective-permute-start | bytes 12296 | tf_op jit(solution)/shard_map/ppermute | solution.py:19
  177.8 5.7 %collective-permute-start.2 = (f32[1024,1]{0,1:T(1,128)S(1)}, f32[1024,1]{0,1:T(1,128)S(1)}, u32[]{:S(2)}, u32[]{:S(2)}) collective-permute-start(f32[1024,1]{0,1:T(1,128)S(1)} %collective-permute-done.1), channel_id=1, source_target_pairs={{0,1},{1,2},{2,3},{3,4},{4,5},{5,6},{6,7},{7,8},{8,9},{9,10},{10,1... | collective-permute-start | bytes 12296 | tf_op jit(solution)/shard_map/ppermute | solution.py:17
  177.9 5.7 %collective-permute-start.10 = (f32[1024,1]{0,1:T(1,128)S(1)}, f32[1024,1]{0,1:T(1,128)S(1)}, u32[]{:S(2)}, u32[]{:S(2)}) collective-permute-start(f32[1024,1]{0,1:T(1,128)S(1)} %collective-permute-done.9), channel_id=1, source_target_pairs={{0,15},{1,0},{2,1},{3,2},{4,3},{5,4},{6,5},{7,6},{8,7},{9,8},{10,9... | collective-permute-start | bytes 12296 | tf_op jit(solution)/shard_map/ppermute | solution.py:19
  183.5 5.7 %collective-permute-start.3 = (f32[1024,1]{0,1:T(1,128)S(1)}, f32[1024,1]{0,1:T(1,128)S(1)}, u32[]{:S(2)}, u32[]{:S(2)}) collective-permute-start(f32[1024,1]{0,1:T(1,128)S(1)} %collective-permute-done.2), channel_id=1, source_target_pairs={{0,1},{1,2},{2,3},{3,4},{4,5},{5,6},{6,7},{7,8},{8,9},{9,10},{10,1... | collective-permute-start | bytes 12296 | tf_op jit(solution)/shard_map/ppermute | solution.py:17
  183.6 12.3 %collective-permute-start.11 = (f32[1024,1]{0,1:T(1,128)S(1)}, f32[1024,1]{0,1:T(1,128)S(1)}, u32[]{:S(2)}, u32[]{:S(2)}) collective-permute-start(f32[1024,1]{0,1:T(1,128)S(1)} %collective-permute-done.10), channel_id=1, source_target_pairs={{0,15},{1,0},{2,1},{3,2},{4,3},{5,4},{6,5},{7,6},{8,7},{9,8},{10,9... | collective-permute-start | bytes 12296 | tf_op jit(solution)/shard_map/ppermute | solution.py:19
  189.3 10.9 %collective-permute-start.4 = (f32[1024,1]{0,1:T(1,128)S(1)}, f32[1024,1]{0,1:T(1,128)S(1)}, u32[]{:S(2)}, u32[]{:S(2)}) collective-permute-start(f32[1024,1]{0,1:T(1,128)S(1)} %collective-permute-done.3), channel_id=1, source_target_pairs={{0,1},{1,2},{2,3},{3,4},{4,5},{5,6},{6,7},{7,8},{8,9},{9,10},{10,1... | collective-permute-start | bytes 12296 | tf_op jit(solution)/shard_map/ppermute | solution.py:17
  189.9 29.9 %all-to-all-start.4 = ((bf16[16,1,32]{2,1,0:T(2,128)(2,1)}), bf16[16,1,32]{2,1,0:T(2,128)(2,1)S(1)}, u32[]{:S(2)}, u32[]{:S(2)}) async-start(bf16[16,1,32]{2,1,0:T(2,128)(2,1)} %copy.28), calls=%async_computation.6 | async-start | bytes 16384 | tf_op jit(solution)/shard_map/all_to_all | solution.py:126
  195.9 41.9 %collective-permute-start.12 = (f32[1024,1]{0,1:T(1,128)S(1)}, f32[1024,1]{0,1:T(1,128)S(1)}, u32[]{:S(2)}, u32[]{:S(2)}) collective-permute-start(f32[1024,1]{0,1:T(1,128)S(1)} %collective-permute-done.11), channel_id=1, source_target_pairs={{0,15},{1,0},{2,1},{3,2},{4,3},{5,4},{6,5},{7,6},{8,7},{9,8},{10,9... | collective-permute-start | bytes 12296 | tf_op jit(solution)/shard_map/ppermute | solution.py:19
  200.2 41.9 %collective-permute-start.5 = (f32[1024,1]{0,1:T(1,128)S(1)}, f32[1024,1]{0,1:T(1,128)S(1)}, u32[]{:S(2)}, u32[]{:S(2)}) collective-permute-start(f32[1024,1]{0,1:T(1,128)S(1)} %collective-permute-done.4), channel_id=1, source_target_pairs={{0,1},{1,2},{2,3},{3,4},{4,5},{5,6},{6,7},{7,8},{8,9},{9,10},{10,1... | collective-permute-start | bytes 12296 | tf_op jit(solution)/shard_map/ppermute | solution.py:17
  219.8 59.9 %all-to-all-start.3 = ((bf16[16,32,1024]{2,1,0:T(8,128)(2,1)}), bf16[16,32,1024]{2,1,0:T(8,128)(2,1)S(1)}, u32[]{:S(2)}, u32[]{:S(2)}) async-start(bf16[16,32,1024]{2,1,0:T(8,128)(2,1)} %convert_element_type.111), calls=%async_computation.4 | async-start | bytes 2097152 | tf_op jit(solution)/shard_map/all_to_all | solution.py:125
  225.4 16.7 %copy-start.4 = (bf16[32,32,1024]{2,1,0:T(8,128)(2,1)S(1)}, bf16[32,32,1024]{2,1,0:T(8,128)(2,1)}, u32[]{:S(2)}) copy-start(bf16[32,32,1024]{2,1,0:T(8,128)(2,1)} %all-gather.6.cloned.1.call-done) | copy-start | bytes 6291460
  225.4 16.7 %copy-start.5 = (bf16[1024,2048]{1,0:T(8,128)(2,1)S(1)}, bf16[1024,2048]{1,0:T(8,128)(2,1)}, u32[]{:S(2)}) copy-start(bf16[1024,2048]{1,0:T(8,128)(2,1)} %get-tuple-element.12) | copy-start | bytes 12582916
  237.8 10.5 %collective-permute-start.13 = (f32[1024,1]{0,1:T(1,128)S(1)}, f32[1024,1]{0,1:T(1,128)S(1)}, u32[]{:S(2)}, u32[]{:S(2)}) collective-permute-start(f32[1024,1]{0,1:T(1,128)S(1)} %collective-permute-done.12), channel_id=1, source_target_pairs={{0,15},{1,0},{2,1},{3,2},{4,3},{5,4},{6,5},{7,6},{8,7},{9,8},{10,9... | collective-permute-start | bytes 12296 | tf_op jit(solution)/shard_map/ppermute | solution.py:19
  242.2 10.6 %collective-permute-start.6 = (f32[1024,1]{0,1:T(1,128)S(1)}, f32[1024,1]{0,1:T(1,128)S(1)}, u32[]{:S(2)}, u32[]{:S(2)}) collective-permute-start(f32[1024,1]{0,1:T(1,128)S(1)} %collective-permute-done.5), channel_id=1, source_target_pairs={{0,1},{1,2},{2,3},{3,4},{4,5},{5,6},{6,7},{7,8},{8,9},{9,10},{10,1... | collective-permute-start | bytes 12296 | tf_op jit(solution)/shard_map/ppermute | solution.py:17
  248.3 30.4 %collective-permute-start.14 = (f32[1024,1]{0,1:T(1,128)S(1)}, f32[1024,1]{0,1:T(1,128)S(1)}, u32[]{:S(2)}, u32[]{:S(2)}) collective-permute-start(f32[1024,1]{0,1:T(1,128)S(1)} %collective-permute-done.13), channel_id=1, source_target_pairs={{0,15},{1,0},{2,1},{3,2},{4,3},{5,4},{6,5},{7,6},{8,7},{9,8},{10,9... | collective-permute-start | bytes 12296 | tf_op jit(solution)/shard_map/ppermute | solution.py:19
  252.7 26.0 %collective-permute-start.7 = (f32[1024,1]{0,1:T(1,128)S(1)}, f32[1024,1]{0,1:T(1,128)S(1)}, u32[]{:S(2)}, u32[]{:S(2)}) collective-permute-start(f32[1024,1]{0,1:T(1,128)S(1)} %collective-permute-done.6), channel_id=1, source_target_pairs={{0,1},{1,2},{2,3},{3,4},{4,5},{5,6},{6,7},{7,8},{8,9},{9,10},{10,1... | collective-permute-start | bytes 12296 | tf_op jit(solution)/shard_map/ppermute | solution.py:17
  252.8 31.9 %copy-start.2 = (bf16[256,1024]{1,0:T(8,128)(2,1)S(1)}, bf16[256,1024]{1,0:T(8,128)(2,1)}, u32[]{:S(2)}) copy-start(bf16[256,1024]{1,0:T(8,128)(2,1)} %param.7) | copy-start | bytes 1572868
Sparse Core Ops, SparseCore 0:
  66.4 33.4 all-gather.5
  101.4 33.1 all-gather.3
  149.9 9.9 reduce-scatter.4
  162.6 54.3 reduce-scatter.2
